TPU v7x, 512 devices: a whole 4x8x8 slice. The times are simulated.
512 devices in a mesh: src: 4 (over z_lo), shard: 16 (over y, core), slab: 8 (over z_hi, x).
Axes of the slice: x: 4, y: 8, z: 8 (z_hi: 2, z_lo: 4; z = z_hi * 4 + z_lo), core: 2. Of those that a mesh axis runs over, the one named last changes fastest.
Arguments:
- src_feat: bfloat16 [4, 256, 256, 256], P('src', 'slab', 'shard'), may hold values from -6 to 6
- coords: int32 [4, 2], P('src'), may hold values from 0 to 6
- offsets: int32 [8], P('slab'), may hold values from 0 to 2128
- weights: bfloat16 [4, 2, 9, 512, 128], P('src'), may hold values from -0.09375 to 0.09375
Outputs:
- target_feat: bfloat16 [4, 256, 256, 256], P('src', 'slab', 'shard')
All inputs are finite; a program needn't handle non-finite values.
Results may differ from a plain program's by a relative error of at most 0.0047.
Values may be sent and summed in bfloat16 or wider, within the bound.
A program may use at most 64 MiB of HBM per device.

v0:
```python
import math
import jax
import jax.numpy as jnp
from jax import lax
from jax.sharding import PartitionSpec as P


def with_halo(shard, sides, width):
    for axis, dim in sides:
        size, length = (lax.axis_size(axis), shard.shape[dim])
        up = [(i, (i + 1) % size) for i in range(size - 1)]
        down = [(j, i) for i, j in up]
        last = lax.slice_in_dim(shard, length - width, length, axis=dim)
        leading = lax.slice_in_dim(shard, 0, width, axis=dim)
        before = lax.ppermute(last, axis, up)
        after = lax.ppermute(leading, axis, down)
        shard = jnp.concatenate([before, shard, after], axis=dim)
    return shard


def encoding(rowpos, chan_count):
    channel_idx = jnp.arange(chan_count, dtype=jnp.int32)
    halves = (channel_idx // 2).astype(jnp.float32)
    frequency = jnp.exp(-math.log(1000.0) * halves / (chan_count / 2))
    phases = (channel_idx % 2).astype(jnp.float32) * (math.pi / 2)
    return jnp.sin(rowpos.astype(jnp.float32)[:, None] * frequency[None, :] + phases[None, :])


def blend_weights(coords):
    vertical = coords[:, 0].astype(jnp.float32) / 6.0
    across = coords[:, 1].astype(jnp.float32) / 6.0
    return jnp.stack(
        [
            (1.0 - vertical) * (1.0 - across),
            (1.0 - vertical) * across,
            vertical * (1.0 - across),
            vertical * across,
        ],
        axis=1,
    )


def local(src_feat, coords, offsets, weights):
    row_count = src_feat.shape[1]
    col_count = src_feat.shape[2]
    chan_count = src_feat.shape[3]
    rowpos = offsets[0] + jnp.arange(row_count, dtype=jnp.int32)
    encoded = encoding(rowpos, chan_count)
    posed = (src_feat.astype(jnp.float32) + encoded[None, :, None, :]).astype(jnp.bfloat16)
    all_views = lax.all_gather(posed, "src", axis=0, tiled=True)
    padded = with_halo(all_views, (("shard", 2), ("slab", 1)), 1)
    view_count = padded.shape[0]
    targets = weights.shape[0]
    groups = weights.shape[1]
    out_width = weights.shape[4]
    per_group = view_count // groups
    grouped = padded.reshape(groups, per_group, row_count + 2, col_count + 2, chan_count)
    grouped = grouped.transpose(0, 2, 3, 1, 4).reshape(
        groups, row_count + 2, col_count + 2, per_group * chan_count
    )
    convolved = jnp.zeros((targets, groups, row_count, col_count, out_width), jnp.float32)
    for tap_index in range(9):
        tap_row = tap_index // 3
        tap_col = tap_index % 3
        window = grouped[:, tap_row : tap_row + row_count, tap_col : tap_col + col_count, :]
        convolved = convolved + jnp.einsum(
            "grcn,tgno->tgrco", window, weights[:, :, tap_index], preferred_element_type=jnp.float32
        )
    convolved = convolved.transpose(0, 2, 3, 1, 4).reshape(
        targets, row_count, col_count, groups * out_width
    )
    mixing = blend_weights(coords)
    own_views = padded[:, 1:-1, 1:-1, :]
    blended = jnp.zeros((targets, row_count, col_count, chan_count), jnp.float32)
    for view_index in range(view_count):
        blended = (
            blended
            + mixing[:, view_index, None, None, None]
            * own_views[view_index].astype(jnp.float32)[None]
        )
    return (blended + jax.nn.silu(convolved)).astype(jnp.bfloat16)


def solution(mesh):
    in_specs = (
        P("src", "slab", "shard", None),
        P("src", None),
        P("slab"),
        P("src", None, None, None, None),
    )
    out_specs = P("src", "slab", "shard", None)
    return jax.shard_map(local, mesh=mesh, in_specs=in_specs, out_specs=out_specs, check_vma=False)
```

profile of v0, /device:TPU:31, one launch (start us, length us, event | category | flops | bytes accessed | tf_op | source)
XLA Modules:
  0.0 106.5 jit_solution(3161733872161110373)
XLA Ops:
  7.2 0.2 add_sine_fusion
  7.4 1.7 %add_convert_fusion.1 = bf16[1,32,16,256]{3,2,1,0:T(8,128)(2,1)} fusion(bf16[1,32,16,256]{3,2,1,0:T(8,128)(2,1)} %param.4, f32[32,256]{1,0:T(8,128)S(1)} %add_sine_fusion), kind=kLoop, calls=%fused_computation.22 | loop fusion | flops 393216 | bytes 557056 | tf_op jit(solution)/shard_map/convert_element_type | solution.py:49
  9.1 0.0 all-gather.2.cloned.1.call-update
  9.1 41.0 %all-gather.2.cloned.1.call-done = bf16[4,32,16,256]{3,2,1,0:T(8,128)(2,1)} async-done(((bf16[1,32,16,256]{3,2,1,0:T(8,128)(2,1)}), bf16[4,32,16,256]{3,2,1,0:T(8,128)(2,1)}) %all-gather.2.cloned.1.call-update) | async-done | bytes 1048592 | tf_op jit(solution)/shard_map/all_gather | solution.py:50
  50.2 1.5 %fusion.37 = (bf16[4,32,1,256]{3,2,1,0:T(2,128)(2,1)S(1)}, bf16[4,32,1,256]{3,2,1,0:T(2,128)(2,1)S(1)}) fusion(bf16[4,32,16,256]{3,2,1,0:T(8,128)(2,1)} %all-gather.2.cloned.1.call-done), kind=kLoop, calls=%fused_computation.59 | loop fusion | bytes 262144 | tf_op jit(solution)/shard_map/slice | solution.py:13
  51.7 5.1 %collective-permute-start = (bf16[4,32,1,256]{3,2,1,0:T(2,128)(2,1)S(1)}, bf16[4,32,1,256]{3,2,1,0:T(2,128)(2,1)S(1)}, u32[]{:S(2)}, u32[]{:S(2)}) collective-permute-start(bf16[4,32,1,256]{3,2,1,0:T(2,128)(2,1)S(1)} %get-tuple-element.16), channel_id=1, source_target_pairs={{0,8},{8,16},{16,24},{24,32},{32,40},{40,48},{48,56},{56,64},{64,7... | collective-permute-start | bytes 196616 | tf_op jit(solution)/shard_map/ppermute | solution.py:15
  56.8 1.9 %collective-permute-start.1 = (bf16[4,32,1,256]{3,2,1,0:T(2,128)(2,1)S(1)}, bf16[4,32,1,256]{3,2,1,0:T(2,128)(2,1)S(1)}, u32[]{:S(2)}, u32[]{:S(2)}) collective-permute-start(bf16[4,32,1,256]{3,2,1,0:T(2,128)(2,1)S(1)} %get-tuple-element.17), channel_id=1, source_target_pairs={{8,0},{16,8},{24,16},{32,24},{40,32},{48,40},{56,48},{64,56},{72,6... | collective-permute-start | bytes 196616 | tf_op jit(solution)/shard_map/ppermute | solution.py:16
  58.7 0.0 collective-permute-done
  58.7 5.6 %collective-permute-done.1 = bf16[4,32,1,256]{3,2,1,0:T(2,128)(2,1)S(1)} collective-permute-done((bf16[4,32,1,256]{3,2,1,0:T(2,128)(2,1)S(1)}, bf16[4,32,1,256]{3,2,1,0:T(2,128)(2,1)S(1)}, u32[]{:S(2)}, u32[]{:S(2)}) %collective-permute-start.1) | collective-permute-done | bytes 65568 | tf_op jit(solution)/shard_map/ppermute | solution.py:16
  64.3 0.8 pad_maximum_fusion.3
  65.1 5.3 %collective-permute-start.2 = (bf16[4,1,18,256]{3,2,1,0:T(8,128)(2,1)S(1)}, bf16[4,1,18,256]{3,2,1,0:T(8,128)(2,1)S(1)}, u32[]{:S(2)}, u32[]{:S(2)}) collective-permute-start(bf16[4,1,18,256]{3,2,1,0:T(8,128)(2,1)S(1)} %get-tuple-element.5), channel_id=1, source_target_pairs={{0,1},{1,2},{2,3},{3,4},{4,5},{5,6},{6,7},{8,9},{9,10},{10,11},{11... | collective-permute-start | bytes 110600 | tf_op jit(solution)/shard_map/ppermute | solution.py:15
  70.4 1.9 %collective-permute-start.3 = (bf16[4,1,18,256]{3,2,1,0:T(8,128)(2,1)S(1)}, bf16[4,1,18,256]{3,2,1,0:T(8,128)(2,1)S(1)}, u32[]{:S(2)}, u32[]{:S(2)}) collective-permute-start(bf16[4,1,18,256]{3,2,1,0:T(8,128)(2,1)S(1)} %get-tuple-element.6), channel_id=1, source_target_pairs={{1,0},{2,1},{3,2},{4,3},{5,4},{6,5},{7,6},{9,8},{10,9},{11,10},{12... | collective-permute-start | bytes 110600 | tf_op jit(solution)/shard_map/ppermute | solution.py:16
  72.3 0.6 fusion.38
  74.3 0.0 collective-permute-done.2
  74.3 7.0 %collective-permute-done.3 = bf16[4,1,18,256]{3,2,1,0:T(8,128)(2,1)S(1)} collective-permute-done((bf16[4,1,18,256]{3,2,1,0:T(8,128)(2,1)S(1)}, bf16[4,1,18,256]{3,2,1,0:T(8,128)(2,1)S(1)}, u32[]{:S(2)}, u32[]{:S(2)}) %collective-permute-start.3) | collective-permute-done | bytes 36896 | tf_op jit(solution)/shard_map/ppermute | solution.py:16
  81.2 1.1 %pad_maximum_fusion = bf16[4,34,18,256]{3,2,1,0:T(8,128)(2,1)S(1)} fusion(bf16[4,1,18,256]{3,2,1,0:T(8,128)(2,1)S(1)} %collective-permute-done.3, bf16[4,32,1,256]{3,2,1,0:T(2,128)(2,1)S(1)} %collective-permute-done.1, bf16[4,32,16,256]{3,2,1,0:T(8,128)(2,1)S(1)} %copy-done, bf16[4,32,1,256]{3,2,1,0:T(2,128)(2,1)S(1)} %collective-permute-done, ...), kind=kLoop, calls=%fused_computation | loop fusion | flops 6266880 | bytes 2506752 | tf_op jit(solution)/shard_map/concatenate | solution.py:17
  82.3 1.0 copy.130
  83.3 0.8 reshape.201
  84.2 0.0 copy-start.1
  84.2 10.1 %fusion.36 = (bf16[2,32,16,512]{3,0,2,1:T(2,128)(2,1)S(1)}, bf16[2,32,16,512]{3,0,2,1:T(2,128)(2,1)S(1)}, bf16[2,32,16,512]{3,0,2,1:T(2,128)(2,1)S(1)}, bf16[2,3...) fusion(bf16[2,34,18,512]{3,0,2,1:T(2,128)(2,1)S(1)} %reshape.201), kind=kLoop, calls=%fused_computation.58 | loop fusion | bytes 18874368 | tf_op jit(solution)/shard_map/slice | solution.py:65
  94.2 0.0 copy-done.1
  94.2 0.4 fusion.9
  94.7 0.4 convolution_add_fusion.7
  95.1 0.4 convolution_add_fusion.6
  95.6 0.4 convolution_add_fusion.5
  96.0 0.4 convolution_add_fusion.4
  96.5 0.4 convolution_add_fusion.3
  96.9 0.4 convolution_add_fusion.2
  97.4 0.4 convolution_add_fusion.1
  97.8 0.4 fusion
  98.3 0.4 copy.80
  98.7 1.0 add_convert_fusion
  (7 shorter events, 0.0 us)
Async XLA Ops:
  6.5 65.8 %copy-start.2 = (s32[1,2]{1,0:T(1,128)S(1)}, s32[1,2]{1,0:T(1,128)}, u32[]{:S(2)}) copy-start(s32[1,2]{1,0:T(1,128)} %param.5) | copy-start | bytes 28
  6.5 43.6 %all-gather.2.cloned.1.call-start = ((), (), s32[]{:S(2)}) async-start(), calls=%async_computation | async-start | bytes 1310720 | tf_op jit(solution)/shard_map/all_gather | solution.py:50
  50.2 31.0 %copy-start = (bf16[4,32,16,256]{3,2,1,0:T(8,128)(2,1)S(1)}, bf16[4,32,16,256]{3,2,1,0:T(8,128)(2,1)}, u32[]{:S(2)}) copy-start(bf16[4,32,16,256]{3,2,1,0:T(8,128)(2,1)} %all-gather.2.cloned.1.call-done) | copy-start | bytes 3145732
  51.7 7.0 %collective-permute-start = (bf16[4,32,1,256]{3,2,1,0:T(2,128)(2,1)S(1)}, bf16[4,32,1,256]{3,2,1,0:T(2,128)(2,1)S(1)}, u32[]{:S(2)}, u32[]{:S(2)}) collective-permute-start(bf16[4,32,1,256]{3,2,1,0:T(2,128)(2,1)S(1)} %get-tuple-element.16), channel_id=1, source_target_pairs={{0,8},{8,16},{16,24},{24,32},{32,40},{40,48},{48,56},{56,64},{64,7... | collective-permute-start | bytes 196616 | tf_op jit(solution)/shard_map/ppermute | solution.py:15
  56.8 7.5 %collective-permute-start.1 = (bf16[4,32,1,256]{3,2,1,0:T(2,128)(2,1)S(1)}, bf16[4,32,1,256]{3,2,1,0:T(2,128)(2,1)S(1)}, u32[]{:S(2)}, u32[]{:S(2)}) collective-permute-start(bf16[4,32,1,256]{3,2,1,0:T(2,128)(2,1)S(1)} %get-tuple-element.17), channel_id=1, source_target_pairs={{8,0},{16,8},{24,16},{32,24},{40,32},{48,40},{56,48},{64,56},{72,6... | collective-permute-start | bytes 196616 | tf_op jit(solution)/shard_map/ppermute | solution.py:16
  65.1 9.1 %collective-permute-start.2 = (bf16[4,1,18,256]{3,2,1,0:T(8,128)(2,1)S(1)}, bf16[4,1,18,256]{3,2,1,0:T(8,128)(2,1)S(1)}, u32[]{:S(2)}, u32[]{:S(2)}) collective-permute-start(bf16[4,1,18,256]{3,2,1,0:T(8,128)(2,1)S(1)} %get-tuple-element.5), channel_id=1, source_target_pairs={{0,1},{1,2},{2,3},{3,4},{4,5},{5,6},{6,7},{8,9},{9,10},{10,11},{11... | collective-permute-start | bytes 110600 | tf_op jit(solution)/shard_map/ppermute | solution.py:15
  70.4 10.9 %collective-permute-start.3 = (bf16[4,1,18,256]{3,2,1,0:T(8,128)(2,1)S(1)}, bf16[4,1,18,256]{3,2,1,0:T(8,128)(2,1)S(1)}, u32[]{:S(2)}, u32[]{:S(2)}) collective-permute-start(bf16[4,1,18,256]{3,2,1,0:T(8,128)(2,1)S(1)} %get-tuple-element.6), channel_id=1, source_target_pairs={{1,0},{2,1},{3,2},{4,3},{5,4},{6,5},{7,6},{9,8},{10,9},{11,10},{12... | collective-permute-start | bytes 110600 | tf_op jit(solution)/shard_map/ppermute | solution.py:16
  84.2 10.1 %copy-start.1 = (bf16[1,2,9,512,128]{4,3,2,1,0:T(8,128)(2,1)S(1)}, bf16[1,2,9,512,128]{4,3,2,1,0:T(8,128)(2,1)}, u32[]{:S(2)}) copy-start(bf16[1,2,9,512,128]{4,3,2,1,0:T(8,128)(2,1)} %param.7) | copy-start | bytes 7077892
Sparse Core Ops, SparseCore 0:
  9.5 40.6 all-gather.1
where the time goes:
time: 107 us
  waiting for transfers between devices  53.6 us (50%)
  between operations  15.6 us (15%)
  local copies, waits for them, and re-layouts  14.4 us (13%)
  starting transfers between devices  14.2 us (13%)
  other arithmetic  4.85 us (5%)
  matrix products  3.96 us (4%)
    all_gather x1, waiting for transfers between devices, local(): all_views = lax.all_gather(posed, 'src', axis=0, tiled=True)  41 us
    ppermute x2, waiting for transfers between devices, with_halo(): after = lax.ppermute(leading, axis, down)  12.5 us
    ppermute x2, starting transfers between devices, with_halo(): before = lax.ppermute(last, axis, up)  10.4 us
    slice x1, local copies, waits for them, and re-layouts, local(): grouped[:, tap_row:tap_row + row_count, tap_col:tap_col + col_count, :]  10.1 us
    dot_general x9, matrix products, local(): jnp.einsum('grcn,tgno->tgrco', window, weights[:, :, tap_index], preferre...  3.96 us
    ppermute x2, starting transfers between devices, with_halo(): after = lax.ppermute(leading, axis, down)  3.84 us
  transfers between devices with their start and end apart: 5, of which 3 were waited for; matrix products, arithmetic and copies ran while one was open for 1% of the time, Pallas kernels for 0%

commit v1 on v0

--- a/solution.py
+++ b/solution.py
@@ -47,7 +47,10 @@
     rowpos = offsets[0] + jnp.arange(row_count, dtype=jnp.int32)
     encoded = encoding(rowpos, chan_count)
     posed = (src_feat.astype(jnp.float32) + encoded[None, :, None, :]).astype(jnp.bfloat16)
-    all_views = lax.all_gather(posed, "src", axis=0, tiled=True)
+    all_views = jnp.concatenate(
+        lax.all_to_all(jnp.stack(tuple((posed for _ in range(lax.axis_size("src"))))), "src", 0, 0),
+        axis=0,
+    )
     padded = with_halo(all_views, (("shard", 2), ("slab", 1)), 1)
     view_count = padded.shape[0]
     targets = weights.shape[0]

time: 107 us -> 84.9 us (0.79)
  waiting for transfers between devices: 53.6 us -> 12.6 us
  blocking collectives: 0 us -> 31.7 us
  between operations: 15.6 us -> 2.15 us
  starting transfers between devices: 14.2 us -> 17.8 us
  other arithmetic: 4.85 us -> 3.37 us
  local copies, waits for them, and re-layouts: 14.4 us -> 13.1 us
    all_gather x1 -> x0, waiting for transfers between devices: 41 us -> none  [local(): all_views = lax.all_gather(posed, 'src', axis=0, tiled=True)]
    all_to_all x0 -> x1, blocking collectives: none -> 31.7 us  [local(): lax.all_to_all(jnp.stack(tuple((posed for _ in range(lax.axis_size('src')...]
    ppermute x2, starting transfers between devices: 10.4 us -> 14 us  [with_halo(): before = lax.ppermute(last, axis, up)]
    slice x1, local copies, waits for them, and re-layouts: 1.49 us -> 0.21 us  [with_halo(): last = lax.slice_in_dim(shard, length - width, length, axis=dim)]
  transfers between devices with their start and end apart: 5 -> 4, of which waited for: 3 -> 2; matrix products, arithmetic and copies ran while one was open for 1% -> 1% of each run, Pallas kernels for 0% -> 0%
where the time goes in v1:
time: 84.9 us; the launch traced here: 84.7 us
  blocking collectives  31.7 us (37%)
  starting transfers between devices  17.8 us (21%)
  local copies, waits for them, and re-layouts  13.1 us (15%)
  waiting for transfers between devices  12.6 us (15%)
  matrix products  3.96 us (5%)
  other arithmetic  3.37 us (4%)
  between operations  2.15 us (3%)
    all_to_all x1, blocking collectives, local(): lax.all_to_all(jnp.stack(tuple((posed for _ in range(lax.axis_size('src')...  31.7 us
    ppermute x2, starting transfers between devices, with_halo(): before = lax.ppermute(last, axis, up)  14 us
    ppermute x2, waiting for transfers between devices, with_halo(): after = lax.ppermute(leading, axis, down)  12.6 us
    slice x1, local copies, waits for them, and re-layouts, local(): grouped[:, tap_row:tap_row + row_count, tap_col:tap_col + col_count, :]  10.1 us
    dot_general x9, matrix products, local(): jnp.einsum('grcn,tgno->tgrco', window, weights[:, :, tap_index], preferre...  3.96 us
    ppermute x2, starting transfers between devices, with_halo(): after = lax.ppermute(leading, axis, down)  3.84 us
  transfers between devices with their start and end apart: 4, of which 2 were waited for; matrix products, arithmetic and copies ran while one was open for 1% of the time, Pallas kernels for 0%

profile of v1, /device:TPU:31, one launch (start us, length us, event | category | flops | bytes accessed | tf_op | source)
XLA Modules:
  0.0 84.7 jit_solution(16379567638602416921)
XLA Ops:
  0.7 0.2 add_sine_fusion
  0.9 1.0 %fusion.12 = bf16[32,16,256]{2,1,0:T(8,128)(2,1)S(1)} fusion(bf16[1,32,16,256]{3,2,1,0:T(8,128)(2,1)} %param.4, f32[32,256]{1,0:T(8,128)S(1)} %add_sine_fusion), kind=kLoop, calls=%fused_computation.24 | loop fusion | flops 393216 | bytes 557056 | tf_op jit(solution)/shard_map/convert_element_type | solution.py:49
  1.9 0.0 copy-start.1
  1.9 0.1 stack.2
  2.0 31.7 %all_to_all.5 = bf16[4,1,32,16,256]{4,3,2,1,0:T(8,128)(2,1)S(1)} all-to-all(bf16[4,1,32,16,256]{4,3,2,1,0:T(8,128)(2,1)S(1)} %stack.2), channel_id=1, replica_groups=mesh['src'=4,'shard'=16,'slab'=8] {'src'}, dimensions={0} | all-to-all | bytes 2097152 | tf_op jit(solution)/shard_map/all_to_all | solution.py:51
  33.6 0.2 fusion.39
  33.8 6.1 %collective-permute-start = (bf16[4,32,1,256]{3,2,1,0:T(2,128)(2,1)S(1)}, bf16[4,32,1,256]{3,2,1,0:T(2,128)(2,1)S(1)}, u32[]{:S(2)}, u32[]{:S(2)}) collective-permute-start(bf16[4,32,1,256]{3,2,1,0:T(2,128)(2,1)S(1)} %get-tuple-element.16), channel_id=1, source_target_pairs={{0,8},{8,16},{16,24},{24,32},{32,40},{40,48},{48,56},{56,64},{64,7... | collective-permute-start | bytes 196616 | tf_op jit(solution)/shard_map/ppermute | solution.py:15
  40.0 1.9 %collective-permute-start.1 = (bf16[4,32,1,256]{3,2,1,0:T(2,128)(2,1)S(1)}, bf16[4,32,1,256]{3,2,1,0:T(2,128)(2,1)S(1)}, u32[]{:S(2)}, u32[]{:S(2)}) collective-permute-start(bf16[4,32,1,256]{3,2,1,0:T(2,128)(2,1)S(1)} %get-tuple-element.17), channel_id=1, source_target_pairs={{8,0},{16,8},{24,16},{32,24},{40,32},{48,40},{56,48},{64,56},{72,6... | collective-permute-start | bytes 196616 | tf_op jit(solution)/shard_map/ppermute | solution.py:16
  41.9 0.0 collective-permute-done
  41.9 5.6 %collective-permute-done.1 = bf16[4,32,1,256]{3,2,1,0:T(2,128)(2,1)S(1)} collective-permute-done((bf16[4,32,1,256]{3,2,1,0:T(2,128)(2,1)S(1)}, bf16[4,32,1,256]{3,2,1,0:T(2,128)(2,1)S(1)}, u32[]{:S(2)}, u32[]{:S(2)}) %collective-permute-start.1) | collective-permute-done | bytes 65568 | tf_op jit(solution)/shard_map/ppermute | solution.py:16
  47.5 7.9 %collective-permute-start.2 = (bf16[4,1,18,256]{3,2,1,0:T(8,128)(2,1)S(1)}, bf16[4,1,18,256]{3,2,1,0:T(8,128)(2,1)S(1)}, u32[]{:S(2)}, u32[]{:S(2)}) collective-permute-start(bf16[4,1,18,256]{3,2,1,0:T(8,128)(2,1)S(1)} %get-tuple-element.5), channel_id=1, source_target_pairs={{0,1},{1,2},{2,3},{3,4},{4,5},{5,6},{6,7},{8,9},{9,10},{10,11},{11... | collective-permute-start | bytes 110600 | tf_op jit(solution)/shard_map/ppermute | solution.py:15
  55.4 1.9 %collective-permute-start.3 = (bf16[4,1,18,256]{3,2,1,0:T(8,128)(2,1)S(1)}, bf16[4,1,18,256]{3,2,1,0:T(8,128)(2,1)S(1)}, u32[]{:S(2)}, u32[]{:S(2)}) collective-permute-start(bf16[4,1,18,256]{3,2,1,0:T(8,128)(2,1)S(1)} %get-tuple-element.6), channel_id=1, source_target_pairs={{1,0},{2,1},{3,2},{4,3},{5,4},{6,5},{7,6},{9,8},{10,9},{11,10},{12... | collective-permute-start | bytes 110600 | tf_op jit(solution)/shard_map/ppermute | solution.py:16
  57.3 0.0 copy-done.1
  57.3 0.6 fusion.40
  59.2 0.0 collective-permute-done.2
  59.2 7.0 %collective-permute-done.3 = bf16[4,1,18,256]{3,2,1,0:T(8,128)(2,1)S(1)} collective-permute-done((bf16[4,1,18,256]{3,2,1,0:T(8,128)(2,1)S(1)}, bf16[4,1,18,256]{3,2,1,0:T(8,128)(2,1)S(1)}, u32[]{:S(2)}, u32[]{:S(2)}) %collective-permute-start.3) | collective-permute-done | bytes 36896 | tf_op jit(solution)/shard_map/ppermute | solution.py:16
  66.2 1.1 %pad_maximum_fusion = bf16[4,34,18,256]{3,2,1,0:T(8,128)(2,1)S(1)} fusion(bf16[4,1,18,256]{3,2,1,0:T(8,128)(2,1)S(1)} %collective-permute-done.3, bf16[4,32,1,256]{3,2,1,0:T(2,128)(2,1)S(1)} %collective-permute-done.1, bf16[4,32,16,256]{3,2,1,0:T(8,128)(2,1)S(1)} %bitcast.111, bf16[4,32,1,256]{3,2,1,0:T(2,128)(2,1)S(1)} %collective-permute-done, ...), kind=kLoop, calls=%fused_computation | loop fusion | flops 6266880 | bytes 2506752 | tf_op jit(solution)/shard_map/concatenate | solution.py:17
  67.3 1.0 %copy.129 = bf16[2,2,34,18,256]{4,1,0,3,2:T(2,128)(2,1)S(1)} copy(bf16[2,2,34,18,256]{4,3,2,1,0:T(8,128)(2,1)S(1)} %bitcast.112) | data formatting | bytes 2506752 | tf_op jit(solution)/shard_map/reshape | solution.py:60
  68.3 0.8 reshape.297
  69.2 0.0 copy-start
  69.2 10.1 %fusion.38 = (bf16[2,32,16,512]{3,0,2,1:T(2,128)(2,1)S(1)}, bf16[2,32,16,512]{3,0,2,1:T(2,128)(2,1)S(1)}, bf16[2,32,16,512]{3,0,2,1:T(2,128)(2,1)S(1)}, bf16[2,3...) fusion(bf16[2,34,18,512]{3,0,2,1:T(2,128)(2,1)S(1)} %reshape.297), kind=kLoop, calls=%fused_computation.60 | loop fusion | bytes 18874368 | tf_op jit(solution)/shard_map/slice | solution.py:68
  79.2 0.4 fusion.9
  79.7 0.4 convolution_add_fusion.7
  80.1 0.4 convolution_add_fusion.6
  80.6 0.4 convolution_add_fusion.5
  81.0 0.4 convolution_add_fusion.4
  81.5 0.4 convolution_add_fusion.3
  81.9 0.4 convolution_add_fusion.2
  82.4 0.4 convolution_add_fusion.1
  82.8 0.4 fusion
  83.2 0.4 copy.79
  83.7 1.0 %fusion.11 = bf16[1,32,16,256]{3,2,1,0:T(8,128)(2,1)} fusion(f32[1,32,16,256]{3,0,2,1:T(1,128)S(1)} %bitcast.114, bf16[4,1,32,16,256]{4,3,2,1,0:T(8,128)(2,1)S(1)} %all_to_all.5, f32[]{:T(128)} %bitcast.7, f32[]{:T(128)} %bitcast.6, f32[]{:T(128)} %bitcast.5, f32[]{:T(128)} %bitcast.2), kind=kLoop, calls=%fused_computation.22 | loop fusion | flops 2228224 | bytes 1835024 | tf_op jit(solution)/shard_map/convert_element_type | solution.py:84
  (4 shorter events, 0.1 us)
Async XLA Ops:
  1.9 55.4 %copy-start.1 = (s32[1,2]{1,0:T(1,128)S(1)}, s32[1,2]{1,0:T(1,128)}, u32[]{:S(2)}) copy-start(s32[1,2]{1,0:T(1,128)} %param.5) | copy-start | bytes 28
  33.8 8.0 %collective-permute-start = (bf16[4,32,1,256]{3,2,1,0:T(2,128)(2,1)S(1)}, bf16[4,32,1,256]{3,2,1,0:T(2,128)(2,1)S(1)}, u32[]{:S(2)}, u32[]{:S(2)}) collective-permute-start(bf16[4,32,1,256]{3,2,1,0:T(2,128)(2,1)S(1)} %get-tuple-element.16), channel_id=1, source_target_pairs={{0,8},{8,16},{16,24},{24,32},{32,40},{40,48},{48,56},{56,64},{64,7... | collective-permute-start | bytes 196616 | tf_op jit(solution)/shard_map/ppermute | solution.py:15
  40.0 7.5 %collective-permute-start.1 = (bf16[4,32,1,256]{3,2,1,0:T(2,128)(2,1)S(1)}, bf16[4,32,1,256]{3,2,1,0:T(2,128)(2,1)S(1)}, u32[]{:S(2)}, u32[]{:S(2)}) collective-permute-start(bf16[4,32,1,256]{3,2,1,0:T(2,128)(2,1)S(1)} %get-tuple-element.17), channel_id=1, source_target_pairs={{8,0},{16,8},{24,16},{32,24},{40,32},{48,40},{56,48},{64,56},{72,6... | collective-permute-start | bytes 196616 | tf_op jit(solution)/shard_map/ppermute | solution.py:16
  47.5 11.7 %collective-permute-start.2 = (bf16[4,1,18,256]{3,2,1,0:T(8,128)(2,1)S(1)}, bf16[4,1,18,256]{3,2,1,0:T(8,128)(2,1)S(1)}, u32[]{:S(2)}, u32[]{:S(2)}) collective-permute-start(bf16[4,1,18,256]{3,2,1,0:T(8,128)(2,1)S(1)} %get-tuple-element.5), channel_id=1, source_target_pairs={{0,1},{1,2},{2,3},{3,4},{4,5},{5,6},{6,7},{8,9},{9,10},{10,11},{11... | collective-permute-start | bytes 110600 | tf_op jit(solution)/shard_map/ppermute | solution.py:15
  55.4 10.9 %collective-permute-start.3 = (bf16[4,1,18,256]{3,2,1,0:T(8,128)(2,1)S(1)}, bf16[4,1,18,256]{3,2,1,0:T(8,128)(2,1)S(1)}, u32[]{:S(2)}, u32[]{:S(2)}) collective-permute-start(bf16[4,1,18,256]{3,2,1,0:T(8,128)(2,1)S(1)} %get-tuple-element.6), channel_id=1, source_target_pairs={{1,0},{2,1},{3,2},{4,3},{5,4},{6,5},{7,6},{9,8},{10,9},{11,10},{12... | collective-permute-start | bytes 110600 | tf_op jit(solution)/shard_map/ppermute | solution.py:16
  69.2 10.1 %copy-start = (bf16[1,2,9,512,128]{4,3,2,1,0:T(8,128)(2,1)S(1)}, bf16[1,2,9,512,128]{4,3,2,1,0:T(8,128)(2,1)}, u32[]{:S(2)}) copy-start(bf16[1,2,9,512,128]{4,3,2,1,0:T(8,128)(2,1)} %param.7) | copy-start | bytes 7077892
